TPU v7x, 128 devices: a whole 4x4x4 slice. The times are simulated.
128 devices in a mesh: row: 16 (over z, y), col: 8 (over x, core).
Axes of the slice: x: 4, y: 4, z: 4, core: 2. Of those that a mesh axis runs over, the one named last changes fastest.
Arguments:
- features: float32 [65536, 512], P(('row', 'col')), may hold values from -6 to 6
- tiles: float32 [16, 8, 128, 128, 128], P('row', 'col'), may hold values from -0.4 to 0.4
- tile_rows: int32 [16, 8, 128], P('row', 'col'), may hold values from 0 to 31
- tile_cols: int32 [16, 8, 128], P('row', 'col'), may hold values from 0 to 31
- tile_count: int32 [16, 8], P('row', 'col'), may hold values from 16 to 128, as said below
- needed: int32 [16, 8, 16, 2], P('row', 'col'), may hold values from 0 to 3, as said below
- w_in: bfloat16 [512, 2048], replicated, may hold values from -0.25 to 0.25
- bias_in: float32 [2048], replicated, may hold values from -5 to 5
- w_out: bfloat16 [2048, 512], replicated, may hold values from -0.125 to 0.125
- bias_out: float32 [512], replicated, may hold values from -5 to 5
Outputs:
- updated: bfloat16 [65536, 512], P(('row', 'col'))
Inputs may be any that keep to these rules, and one draw needn't show every extreme that they name: tile_count of every grid cell lies between 16 and 64, except one cell of each draw that has all 128 tiles live. Each list needed[r, c, q] holds 2 different block numbers.
All inputs are finite; a program needn't handle non-finite values.
Results may differ from a plain program's by a relative error of at most 0.0054.
Values sent between devices are 32-bit elements; how exact they have to be, the bound alone decides.
No kernel may reach another device: no remote copies, remote signals or barrier semaphores. Data moves between devices by JAX's collectives and lax.ppermute only.
A program may use at most 128 MiB of HBM per device.

v0:
```python
import math
import jax
import jax.numpy as jnp
from jax import lax
from jax.sharding import PartitionSpec as P

gin_epsilon = 0.25
precise_mode = lax.Precision.HIGHEST


def on_device(
    features, tiles, tile_rows, tile_cols, tile_count, needed, w_in, bias_in, w_out, bias_out
):
    tile_edge = tiles.shape[-1]
    width = features.shape[1]
    blocks_dev = features.shape[0] // tile_edge
    grid_cols = lax.axis_size("col")
    slot_count = needed.shape[-1]
    own_blocks = features.reshape(blocks_dev, tile_edge, width)
    my_tiles = tiles[0, 0]
    tile_row = tile_rows[0, 0]
    tile_col = tile_cols[0, 0]
    wanted = needed[0, 0]
    column_pool = lax.all_gather(own_blocks, "row", axis=0, tiled=True)
    source = tile_col // slot_count
    position = source * blocks_dev + jnp.take(wanted.reshape(-1), tile_col)
    tile_total = my_tiles.shape[0]
    group = math.gcd(32, tile_total)
    row_blocks = grid_cols * blocks_dev
    live = (jnp.arange(tile_total) < tile_count[0, 0]).astype(jnp.float32)
    block_ids = jnp.arange(row_blocks, dtype=jnp.int32)

    def add_group(turn, partial_value):
        start = turn * group
        group_tiles = lax.dynamic_slice_in_dim(my_tiles, start, group, 0)
        group_pos = lax.dynamic_slice_in_dim(position, start, group, 0)
        group_row = lax.dynamic_slice_in_dim(tile_row, start, group, 0)
        group_live = lax.dynamic_slice_in_dim(live, start, group, 0)
        inputs = jnp.take(column_pool, group_pos, axis=0)
        product = jnp.einsum("tpq,tqf->tpf", group_tiles, inputs, precision=precise_mode)
        selector = (group_row[None, :] == block_ids[:, None]).astype(jnp.float32) * group_live[
            None, :
        ]
        return partial_value + jnp.dot(
            selector, product.reshape(group, tile_edge * width), precision=precise_mode
        )

    partial_value = lax.fori_loop(
        0, tile_total // group, add_group, jnp.zeros((row_blocks, tile_edge * width), jnp.float32)
    )
    summed = lax.psum_scatter(
        partial_value.reshape(row_blocks * tile_edge, width), "col", scatter_dimension=0, tiled=True
    )
    mixed = ((1.0 + gin_epsilon) * features + summed).astype(jnp.bfloat16)
    hidden = jax.nn.relu(jnp.dot(mixed, w_in, preferred_element_type=jnp.float32) + bias_in).astype(
        jnp.bfloat16
    )
    return (jnp.dot(hidden, w_out, preferred_element_type=jnp.float32) + bias_out).astype(
        jnp.bfloat16
    )


def solution(mesh):
    placed = (
        P(("row", "col"), None),
        P("row", "col", None, None, None),
        P("row", "col", None),
        P("row", "col", None),
        P("row", "col"),
        P("row", "col", None, None),
        P(),
        P(),
        P(),
        P(),
    )
    return jax.shard_map(
        on_device, mesh=mesh, in_specs=placed, out_specs=P(("row", "col"), None), check_vma=False
    )
```

profile of v0, /device:TPU:1, one launch (start us, length us, event | category | flops | bytes accessed | tf_op | source)
XLA Modules:
  0.0 363.8 jit_solution(9578048227056878667)
XLA Ops:
  6.5 0.0 copy-start
  6.5 0.7 all-gather.2.cloned.1.call-update
  7.3 0.0 reduce-scatter.2.cloned.1.call-start
  7.3 0.8 copy.13
  8.1 0.1 reshape_squeeze.3
  8.8 0.7 fusion.18
  9.5 1.2 gather_fusion.1
  10.7 0.7 fusion.17
  11.4 112.5 %all-gather.2.cloned.1.call-done = f32[64,128,512]{2,1,0:T(8,128)} async-done(((f32[4,128,512]{2,1,0:T(8,128)}), f32[64,128,512]{2,1,0:T(8,128)}) %all-gather.2.cloned.1.call-update) | async-done | bytes 16777232 | tf_op jit(solution)/shard_map/all_gather | solution.py:24
  123.9 168.7 %while.14 = (s32[]{:T(128)}, f32[32,65536]{1,0:T(8,128)}, s32[128]{0:T(128)}, f32[128]{0:T(128)S(1)}, f32[128,128,128]{2,1,0:T(8,128)}, /*index=5*/s32[128]{0:T(...) while((s32[]{:T(128)}, f32[32,65536]{1,0:T(8,128)}, ...), condition=%wide.region_1.2_spmd.clone, body=%wide.region_0.1_spmd.clone.sunk | while | flops 4032826624 | bytes 77602320 | solution.py:48
  123.9 0.1 compare_and_fusion.2
  124.0 10.1 %gather_fusion = f32[32,128,512]{2,1,0:T(8,128)} fusion(f32[64,128,512]{2,1,0:T(8,128)} %get-tuple-element.262, s32[1024]{0:T(1024)S(1)} %pad_clamp_fusion.3), kind=kCustom, calls=%fused_computation.clone.clone.1 | custom fusion | bytes 16777344 | tf_op jit(solution)/shard_map/while/body/eval_jaxpr/jit(_take)/gather | solution.py:39
  134.0 10.9 %fusion.34 = f32[32,128,512]{2,1,0:T(8,128)S(1)} fusion(f32[32,128,512]{2,1,0:T(8,128)} %gather_fusion, pred[32]{0:T(512)(128)(4,1)S(1)} %get-tuple-element.233, f32[128,128,128]{2,1,0:T(8,128)} %get-tuple-element.260, s32[]{:T(128)S(6)} %select_n.79), kind=kOutput, calls=%fused_computation.4.clone.1 | convolution fusion | flops 3223322624 | bytes 18874404 | tf_op jit(solution)/shard_map/while/body/eval_jaxpr/tpq,tqf->tpf/dot_general | solution.py:40
  145.0 0.0 copy-start.4
  145.0 8.1 %copy.16 = f32[4,8,128,512]{3,1,2,0:T(8,128)} copy(f32[4,8,128,512]{3,2,1,0:T(8,128)S(1)} %bitcast.33) | data formatting | bytes 16777216 | tf_op jit(solution)/shard_map/while
  153.1 0.1 dynamic_slice.40
  153.1 0.0 copy-done.4
  153.1 0.1 dynamic_slice.41
  153.2 11.9 %convolution_add_fusion.3 = f32[32,65536]{1,0:T(8,128)} fusion(f32[32,65536]{1,0:T(8,128)} %bitcast.34, f32[32,65536]{1,0:T(8,128)} %get-tuple-element.246, pred[]{:T(512)S(6)} %compare.5, f32[32]{0:T(128)S(1)} %dynamic_slice.40, s32[32]{0:T(128)S(1)} %dynamic_slice.41), kind=kOutput, calls=%fused_computation.3.clone.1 | convolution fusion | flops 809502720 | bytes 25166080 | tf_op jit(solution)/shard_map/while/body/eval_jaxpr/dot_general | solution.py:44
  165.1 0.1 compare_and_fusion.2
  165.2 10.1 %gather_fusion = f32[32,128,512]{2,1,0:T(8,128)} fusion(f32[64,128,512]{2,1,0:T(8,128)} %get-tuple-element.262, s32[1024]{0:T(1024)S(1)} %pad_clamp_fusion.3), kind=kCustom, calls=%fused_computation.clone.clone.1 | custom fusion | bytes 16777344 | tf_op jit(solution)/shard_map/while/body/eval_jaxpr/jit(_take)/gather | solution.py:39
  175.3 10.9 %fusion.34 = f32[32,128,512]{2,1,0:T(8,128)S(1)} fusion(f32[32,128,512]{2,1,0:T(8,128)} %gather_fusion, pred[32]{0:T(512)(128)(4,1)S(1)} %get-tuple-element.233, f32[128,128,128]{2,1,0:T(8,128)} %get-tuple-element.260, s32[]{:T(128)S(6)} %select_n.79), kind=kOutput, calls=%fused_computation.4.clone.1 | convolution fusion | flops 3223322624 | bytes 18874404 | tf_op jit(solution)/shard_map/while/body/eval_jaxpr/tpq,tqf->tpf/dot_general | solution.py:40
  186.2 0.0 copy-start.4
  186.2 8.1 %copy.16 = f32[4,8,128,512]{3,1,2,0:T(8,128)} copy(f32[4,8,128,512]{3,2,1,0:T(8,128)S(1)} %bitcast.33) | data formatting | bytes 16777216 | tf_op jit(solution)/shard_map/while
  194.3 0.1 dynamic_slice.40
  194.3 0.1 dynamic_slice.41
  194.4 13.2 %convolution_add_fusion.3 = f32[32,65536]{1,0:T(8,128)} fusion(f32[32,65536]{1,0:T(8,128)} %bitcast.34, f32[32,65536]{1,0:T(8,128)} %get-tuple-element.246, pred[]{:T(512)S(6)} %compare.5, f32[32]{0:T(128)S(1)} %dynamic_slice.40, s32[32]{0:T(128)S(1)} %dynamic_slice.41), kind=kOutput, calls=%fused_computation.3.clone.1 | convolution fusion | flops 809502720 | bytes 25166080 | tf_op jit(solution)/shard_map/while/body/eval_jaxpr/dot_general | solution.py:44
  207.6 0.1 compare_and_fusion.2
  207.7 10.1 %gather_fusion = f32[32,128,512]{2,1,0:T(8,128)} fusion(f32[64,128,512]{2,1,0:T(8,128)} %get-tuple-element.262, s32[1024]{0:T(1024)S(1)} %pad_clamp_fusion.3), kind=kCustom, calls=%fused_computation.clone.clone.1 | custom fusion | bytes 16777344 | tf_op jit(solution)/shard_map/while/body/eval_jaxpr/jit(_take)/gather | solution.py:39
  217.8 10.9 %fusion.34 = f32[32,128,512]{2,1,0:T(8,128)S(1)} fusion(f32[32,128,512]{2,1,0:T(8,128)} %gather_fusion, pred[32]{0:T(512)(128)(4,1)S(1)} %get-tuple-element.233, f32[128,128,128]{2,1,0:T(8,128)} %get-tuple-element.260, s32[]{:T(128)S(6)} %select_n.79), kind=kOutput, calls=%fused_computation.4.clone.1 | convolution fusion | flops 3223322624 | bytes 18874404 | tf_op jit(solution)/shard_map/while/body/eval_jaxpr/tpq,tqf->tpf/dot_general | solution.py:40
  228.7 0.0 copy-start.4
  228.7 8.1 %copy.16 = f32[4,8,128,512]{3,1,2,0:T(8,128)} copy(f32[4,8,128,512]{3,2,1,0:T(8,128)S(1)} %bitcast.33) | data formatting | bytes 16777216 | tf_op jit(solution)/shard_map/while
  236.8 0.1 dynamic_slice.40
  236.8 0.1 dynamic_slice.41
  236.9 13.2 %convolution_add_fusion.3 = f32[32,65536]{1,0:T(8,128)} fusion(f32[32,65536]{1,0:T(8,128)} %bitcast.34, f32[32,65536]{1,0:T(8,128)} %get-tuple-element.246, pred[]{:T(512)S(6)} %compare.5, f32[32]{0:T(128)S(1)} %dynamic_slice.40, s32[32]{0:T(128)S(1)} %dynamic_slice.41), kind=kOutput, calls=%fused_computation.3.clone.1 | convolution fusion | flops 809502720 | bytes 25166080 | tf_op jit(solution)/shard_map/while/body/eval_jaxpr/dot_general | solution.py:44
  250.1 0.1 compare_and_fusion.2
  250.2 10.1 %gather_fusion = f32[32,128,512]{2,1,0:T(8,128)} fusion(f32[64,128,512]{2,1,0:T(8,128)} %get-tuple-element.262, s32[1024]{0:T(1024)S(1)} %pad_clamp_fusion.3), kind=kCustom, calls=%fused_computation.clone.clone.1 | custom fusion | bytes 16777344 | tf_op jit(solution)/shard_map/while/body/eval_jaxpr/jit(_take)/gather | solution.py:39
  260.2 10.9 %fusion.34 = f32[32,128,512]{2,1,0:T(8,128)S(1)} fusion(f32[32,128,512]{2,1,0:T(8,128)} %gather_fusion, pred[32]{0:T(512)(128)(4,1)S(1)} %get-tuple-element.233, f32[128,128,128]{2,1,0:T(8,128)} %get-tuple-element.260, s32[]{:T(128)S(6)} %select_n.79), kind=kOutput, calls=%fused_computation.4.clone.1 | convolution fusion | flops 3223322624 | bytes 18874404 | tf_op jit(solution)/shard_map/while/body/eval_jaxpr/tpq,tqf->tpf/dot_general | solution.py:40
  271.2 0.0 copy-start.4
  271.2 8.1 %copy.16 = f32[4,8,128,512]{3,1,2,0:T(8,128)} copy(f32[4,8,128,512]{3,2,1,0:T(8,128)S(1)} %bitcast.33) | data formatting | bytes 16777216 | tf_op jit(solution)/shard_map/while
  279.3 0.1 dynamic_slice.40
  279.3 0.1 dynamic_slice.41
  279.4 13.2 %convolution_add_fusion.3 = f32[32,65536]{1,0:T(8,128)} fusion(f32[32,65536]{1,0:T(8,128)} %bitcast.34, f32[32,65536]{1,0:T(8,128)} %get-tuple-element.246, pred[]{:T(512)S(6)} %compare.5, f32[32]{0:T(128)S(1)} %dynamic_slice.40, s32[32]{0:T(128)S(1)} %dynamic_slice.41), kind=kOutput, calls=%fused_computation.3.clone.1 | convolution fusion | flops 809502720 | bytes 25166080 | tf_op jit(solution)/shard_map/while/body/eval_jaxpr/dot_general | solution.py:44
  292.6 7.5 %reshape.58 = f32[4096,512]{1,0:T(8,128)} reshape(f32[32,65536]{1,0:T(8,128)} %get-tuple-element.144) | data formatting | bytes 16777216 | tf_op jit(solution)/shard_map/reshape | solution.py:52
  300.1 0.0 reduce-scatter.2.cloned.1.call-update
  300.1 51.8 %reduce-scatter.2.cloned.1.call-done = f32[512,512]{1,0:T(8,128)} async-done(((f32[4096,512]{1,0:T(8,128)}), f32[512,512]{1,0:T(8,128)}) %reduce-scatter.2.cloned.1.call-update) | async-done | bytes 1048592 | tf_op jit(solution)/shard_map/reduce_scatter | solution.py:51
  351.9 0.0 copy-done.1
  351.9 5.1 %fusion.14 = bf16[512,512]{1,0:T(8,128)(2,1)} fusion(bf16[2048,512]{1,0:T(8,128)(2,1)S(1)} %copy-done, bf16[512,2048]{1,0:T(8,128)(2,1)} %param.18, f32[2048]{0:T(1024)S(1)} %copy-done.2, f32[512,512]{1,0:T(8,128)} %reduce-scatter.2.cloned.1.call-done, f32[512,512]{1,0:T(8,128)S(1)} %copy-done.1, f32[512]{0:T(512)S(1)} %copy-done.3), kind=kOutput, calls=%fused_computation.22 | convolution fusion | flops 2151940096 | bytes 6825984 | tf_op jit(solution)/shard_map/dot_general | solution.py:58
  (17 shorter events, 0.1 us)
Async XLA Ops:
  6.5 345.4 %copy-start = (bf16[2048,512]{1,0:T(8,128)(2,1)S(1)}, bf16[2048,512]{1,0:T(8,128)(2,1)}, u32[]{:S(2)}) copy-start(bf16[2048,512]{1,0:T(8,128)(2,1)} %param.20) | copy-start | bytes 6291460
  6.5 117.3 %all-gather.2.cloned.1.call-start = ((), (), s32[]{:S(2)}) async-start(), calls=%async_computation.1 | async-start | bytes 17825792 | tf_op jit(solution)/shard_map/all_gather | solution.py:24
  7.3 344.6 %reduce-scatter.2.cloned.1.call-start = ((), (), s32[]{:S(2)}) async-start(), calls=%async_computation.2 | async-start | bytes 9437184 | tf_op jit(solution)/shard_map/reduce_scatter | solution.py:51
  145.0 8.2 %copy-start.4 = (s32[128]{0:T(128)S(1)}, s32[128]{0:T(128)}, u32[]{:S(2)}) copy-start(s32[128]{0:T(128)} %get-tuple-element.258) | copy-start | bytes 1540 | tf_op jit(solution)/shard_map/while
  186.2 8.2 %copy-start.4 = (s32[128]{0:T(128)S(1)}, s32[128]{0:T(128)}, u32[]{:S(2)}) copy-start(s32[128]{0:T(128)} %get-tuple-element.258) | copy-start | bytes 1540 | tf_op jit(solution)/shard_map/while
  228.7 8.2 %copy-start.4 = (s32[128]{0:T(128)S(1)}, s32[128]{0:T(128)}, u32[]{:S(2)}) copy-start(s32[128]{0:T(128)} %get-tuple-element.258) | copy-start | bytes 1540 | tf_op jit(solution)/shard_map/while
  271.2 8.2 %copy-start.4 = (s32[128]{0:T(128)S(1)}, s32[128]{0:T(128)}, u32[]{:S(2)}) copy-start(s32[128]{0:T(128)} %get-tuple-element.258) | copy-start | bytes 1540 | tf_op jit(solution)/shard_map/while
  300.1 51.8 %copy-start.1 = (f32[512,512]{1,0:T(8,128)S(1)}, f32[512,512]{1,0:T(8,128)}, u32[]{:S(2)}) copy-start(f32[512,512]{1,0:T(8,128)} %param.12) | copy-start | bytes 3145732
  300.1 51.8 %copy-start.2 = (f32[2048]{0:T(1024)S(1)}, f32[2048]{0:T(1024)}, u32[]{:S(2)}) copy-start(f32[2048]{0:T(1024)} %param.19) | copy-start | bytes 24580
  300.1 51.8 %copy-start.3 = (f32[512]{0:T(512)S(1)}, f32[512]{0:T(512)}, u32[]{:S(2)}) copy-start(f32[512]{0:T(512)} %param.21) | copy-start | bytes 6148
Sparse Core Ops, SparseCore 0:
  9.5 114.3 all-gather.1
  300.2 51.6 reduce-scatter.1
where the time goes:
time: 364 us
  waiting for transfers between devices  165 us (45%)
  matrix products  100 us (27%)
  local copies, waits for them, and re-layouts  82.8 us (23%)
  between operations  14.1 us (4%)
    all_gather x1, waiting for transfers between devices, on_device(): column_pool = lax.all_gather(own_blocks, 'row', axis=0, tiled=True)  112 us
    reduce_scatter x1, waiting for transfers between devices, on_device(): lax.psum_scatter(partial_value.reshape(row_blocks * tile_edge, width), 'c...  51.8 us
    dot_general x4, matrix products, add_group(): jnp.dot(selector, product.reshape(group, tile_edge * width), precision=pr...  51.4 us
    dot_general x4, matrix products, add_group(): jnp.einsum('tpq,tqf->tpf', group_tiles, inputs, precision=precise_mode)  43.6 us
    gather x4, local copies, waits for them, and re-layouts, add_group(): inputs = jnp.take(column_pool, group_pos, axis=0)  40.3 us
    while x12, local copies, waits for them, and re-layouts  32.4 us
    reshape x1, local copies, waits for them, and re-layouts, on_device(): partial_value.reshape(row_blocks * tile_edge, width)  7.49 us
  transfers between devices with their start and end apart: 2, of which 2 were waited for; matrix products, arithmetic and copies ran while one was open for 1% of the time, Pallas kernels for 0%

commit v1 on v0

--- a/solution.py
+++ b/solution.py
@@ -21,7 +21,10 @@
     tile_row = tile_rows[0, 0]
     tile_col = tile_cols[0, 0]
     wanted = needed[0, 0]
-    column_pool = lax.all_gather(own_blocks, "row", axis=0, tiled=True)
+    n_dev = lax.axis_size("row")
+    parts = jnp.stack([own_blocks for _ in range(n_dev)])
+    parts = lax.all_to_all(parts, "row", split_axis=0, concat_axis=0)
+    column_pool = jnp.concatenate(parts, axis=0)
     source = tile_col // slot_count
     position = source * blocks_dev + jnp.take(wanted.reshape(-1), tile_col)
     tile_total = my_tiles.shape[0]

time: 364 us -> 513 us (1.41)
  waiting for transfers between devices: 165 us -> 298 us
  starting transfers between devices: 0.04 us -> 8.81 us
  local copies, waits for them, and re-layouts: 82.8 us -> 91.3 us
    all_to_all x0 -> x1, waiting for transfers between devices: none -> 247 us  [on_device(): parts = lax.all_to_all(parts, 'row', split_axis=0, concat_axis=0)]
    all_gather x1 -> x0, waiting for transfers between devices: 112 us -> none  [on_device(): column_pool = lax.all_gather(own_blocks, 'row', axis=0, tiled=True)]
    another operation x0 -> x1, local copies, waits for them, and re-layouts: none -> 9.26 us  [on_device(): parts = jnp.stack([own_blocks for _ in range(n_dev)])]
    all_to_all x0 -> x1, starting transfers between devices: none -> 8.77 us  [on_device(): parts = lax.all_to_all(parts, 'row', split_axis=0, concat_axis=0)]
    while x12 -> x4, local copies, waits for them, and re-layouts: 32.4 us -> 32.3 us
  transfers between devices with their start and end apart: 2 -> 2, of which waited for: 2 -> 2; matrix products, arithmetic and copies ran while one was open for 1% -> 0% of each run, Pallas kernels for 0% -> 0%
where the time goes in v1:
time: 513 us; the launch traced here: 512 us
  waiting for transfers between devices  298 us (58%)
  matrix products  99.9 us (19%)
  local copies, waits for them, and re-layouts  91.3 us (18%)
  between operations  14.1 us (3%)
  starting transfers between devices  8.81 us (2%)
    all_to_all x1, waiting for transfers between devices, on_device(): parts = lax.all_to_all(parts, 'row', split_axis=0, concat_axis=0)  247 us
    dot_general x4, matrix products, add_group(): jnp.dot(selector, product.reshape(group, tile_edge * width), precision=pr...  51.2 us
    reduce_scatter x1, waiting for transfers between devices, on_device(): lax.psum_scatter(partial_value.reshape(row_blocks * tile_edge, width), 'c...  50.8 us
    dot_general x4, matrix products, add_group(): jnp.einsum('tpq,tqf->tpf', group_tiles, inputs, precision=precise_mode)  43.6 us
    gather x4, local copies, waits for them, and re-layouts, add_group(): inputs = jnp.take(column_pool, group_pos, axis=0)  40.3 us
    while x4, local copies, waits for them, and re-layouts  32.3 us
  transfers between devices with their start and end apart: 2, of which 2 were waited for; matrix products, arithmetic and copies ran while one was open for 0% of the time, Pallas kernels for 0%

profile of v1, /device:TPU:1, one launch (start us, length us, event | category | flops | bytes accessed | tf_op | source)
XLA Modules:
  0.0 512.3 jit_solution(9515069803146729856)
XLA Ops:
  6.5 0.0 copy-start
  6.5 9.3 %stack.3 = f32[16,4,128,512]{3,2,1,0:T(8,128)} broadcast(f32[4,128,512]{2,1,0:T(8,128)} %bitcast.37), dimensions={1,2,3} | broadcast | bytes 17825792 | tf_op jit(solution)/shard_map/stack | solution.py:25
  15.8 8.8 %all-to-all-start = ((f32[16,4,128,512]{3,2,1,0:T(8,128)}), f32[16,4,128,512]{3,2,1,0:T(8,128)}, u32[]{:S(2)}, u32[]{:S(2)}) async-start(f32[16,4,128,512]{3,2,1,0:T(8,128)} %stack.3), calls=%async_computation | async-start | bytes 33554432 | tf_op jit(solution)/shard_map/all_to_all | solution.py:26
  24.6 0.0 reduce-scatter.2.cloned.1.call-start
  24.6 0.0 copy-done.2
  24.7 0.1 copy.12
  24.7 0.1 reshape_squeeze.3
  25.5 0.0 copy-done.5
  25.5 1.2 gather_fusion.1
  26.8 246.9 %all-to-all-done = f32[16,4,128,512]{3,2,1,0:T(8,128)} async-done(((f32[16,4,128,512]{3,2,1,0:T(8,128)}), f32[16,4,128,512]{3,2,1,0:T(8,128)}, u32[]{:S(2)}, u32[]{:S(2)}) %all-to-all-start) | async-done | bytes 16777248 | tf_op jit(solution)/shard_map/all_to_all | solution.py:26
  273.7 0.0 copy-done.6
  273.7 168.3 %while.14 = (s32[]{:T(128)}, f32[32,65536]{1,0:T(8,128)}, s32[128]{0:T(128)S(1)}, f32[128]{0:T(128)S(1)}, f32[128,128,128]{2,1,0:T(8,128)}, /*index=5*/s32[128]{...) while((s32[]{:T(128)}, f32[32,65536]{1,0:T(8,128)}, ...), condition=%wide.region_1.2_spmd.clone, body=%wide.region_0.1_spmd.clone.sunk | while | flops 4032826624 | bytes 77600240 | solution.py:51
  273.7 0.1 compare_and_fusion.2
  273.8 10.1 %gather_fusion = f32[32,128,512]{2,1,0:T(8,128)} fusion(f32[64,128,512]{2,1,0:T(8,128)} %get-tuple-element.262, s32[1024]{0:T(1024)S(1)} %pad_clamp_fusion.3), kind=kCustom, calls=%fused_computation.clone.clone.1 | custom fusion | bytes 16777344 | tf_op jit(solution)/shard_map/while/body/eval_jaxpr/jit(_take)/gather | solution.py:42
  283.9 10.9 %fusion.34 = f32[32,128,512]{2,1,0:T(8,128)S(1)} fusion(f32[32,128,512]{2,1,0:T(8,128)} %gather_fusion, pred[32]{0:T(512)(128)(4,1)S(1)} %get-tuple-element.233, f32[128,128,128]{2,1,0:T(8,128)} %get-tuple-element.260, s32[]{:T(128)S(6)} %select_n.79), kind=kOutput, calls=%fused_computation.4.clone.1 | convolution fusion | flops 3223322624 | bytes 18874404 | tf_op jit(solution)/shard_map/while/body/eval_jaxpr/tpq,tqf->tpf/dot_general | solution.py:43
  294.8 8.1 %copy.15 = f32[4,8,128,512]{3,1,2,0:T(8,128)} copy(f32[4,8,128,512]{3,2,1,0:T(8,128)S(1)} %bitcast.34) | data formatting | bytes 16777216 | tf_op jit(solution)/shard_map/while
  302.9 0.1 dynamic_slice.40
  302.9 0.1 dynamic_slice.41
  303.0 11.8 %convolution_add_fusion.3 = f32[32,65536]{1,0:T(8,128)} fusion(f32[32,65536]{1,0:T(8,128)} %bitcast.35, f32[32,65536]{1,0:T(8,128)} %get-tuple-element.246, pred[]{:T(512)S(6)} %compare.5, f32[32]{0:T(128)S(1)} %dynamic_slice.40, s32[32]{0:T(128)S(1)} %dynamic_slice.41), kind=kOutput, calls=%fused_computation.3.clone.1 | convolution fusion | flops 809502720 | bytes 25166080 | tf_op jit(solution)/shard_map/while/body/eval_jaxpr/dot_general | solution.py:47
  314.8 0.1 compare_and_fusion.2
  314.9 10.1 %gather_fusion = f32[32,128,512]{2,1,0:T(8,128)} fusion(f32[64,128,512]{2,1,0:T(8,128)} %get-tuple-element.262, s32[1024]{0:T(1024)S(1)} %pad_clamp_fusion.3), kind=kCustom, calls=%fused_computation.clone.clone.1 | custom fusion | bytes 16777344 | tf_op jit(solution)/shard_map/while/body/eval_jaxpr/jit(_take)/gather | solution.py:42
  325.0 10.9 %fusion.34 = f32[32,128,512]{2,1,0:T(8,128)S(1)} fusion(f32[32,128,512]{2,1,0:T(8,128)} %gather_fusion, pred[32]{0:T(512)(128)(4,1)S(1)} %get-tuple-element.233, f32[128,128,128]{2,1,0:T(8,128)} %get-tuple-element.260, s32[]{:T(128)S(6)} %select_n.79), kind=kOutput, calls=%fused_computation.4.clone.1 | convolution fusion | flops 3223322624 | bytes 18874404 | tf_op jit(solution)/shard_map/while/body/eval_jaxpr/tpq,tqf->tpf/dot_general | solution.py:43
  335.9 8.1 %copy.15 = f32[4,8,128,512]{3,1,2,0:T(8,128)} copy(f32[4,8,128,512]{3,2,1,0:T(8,128)S(1)} %bitcast.34) | data formatting | bytes 16777216 | tf_op jit(solution)/shard_map/while
  344.0 0.1 dynamic_slice.40
  344.1 0.1 dynamic_slice.41
  344.1 13.1 %convolution_add_fusion.3 = f32[32,65536]{1,0:T(8,128)} fusion(f32[32,65536]{1,0:T(8,128)} %bitcast.35, f32[32,65536]{1,0:T(8,128)} %get-tuple-element.246, pred[]{:T(512)S(6)} %compare.5, f32[32]{0:T(128)S(1)} %dynamic_slice.40, s32[32]{0:T(128)S(1)} %dynamic_slice.41), kind=kOutput, calls=%fused_computation.3.clone.1 | convolution fusion | flops 809502720 | bytes 25166080 | tf_op jit(solution)/shard_map/while/body/eval_jaxpr/dot_general | solution.py:47
  357.2 0.1 compare_and_fusion.2
  357.3 10.1 %gather_fusion = f32[32,128,512]{2,1,0:T(8,128)} fusion(f32[64,128,512]{2,1,0:T(8,128)} %get-tuple-element.262, s32[1024]{0:T(1024)S(1)} %pad_clamp_fusion.3), kind=kCustom, calls=%fused_computation.clone.clone.1 | custom fusion | bytes 16777344 | tf_op jit(solution)/shard_map/while/body/eval_jaxpr/jit(_take)/gather | solution.py:42
  367.4 10.9 %fusion.34 = f32[32,128,512]{2,1,0:T(8,128)S(1)} fusion(f32[32,128,512]{2,1,0:T(8,128)} %gather_fusion, pred[32]{0:T(512)(128)(4,1)S(1)} %get-tuple-element.233, f32[128,128,128]{2,1,0:T(8,128)} %get-tuple-element.260, s32[]{:T(128)S(6)} %select_n.79), kind=kOutput, calls=%fused_computation.4.clone.1 | convolution fusion | flops 3223322624 | bytes 18874404 | tf_op jit(solution)/shard_map/while/body/eval_jaxpr/tpq,tqf->tpf/dot_general | solution.py:43
  378.3 8.1 %copy.15 = f32[4,8,128,512]{3,1,2,0:T(8,128)} copy(f32[4,8,128,512]{3,2,1,0:T(8,128)S(1)} %bitcast.34) | data formatting | bytes 16777216 | tf_op jit(solution)/shard_map/while
  386.4 0.1 dynamic_slice.40
  386.5 0.1 dynamic_slice.41
  386.5 13.1 %convolution_add_fusion.3 = f32[32,65536]{1,0:T(8,128)} fusion(f32[32,65536]{1,0:T(8,128)} %bitcast.35, f32[32,65536]{1,0:T(8,128)} %get-tuple-element.246, pred[]{:T(512)S(6)} %compare.5, f32[32]{0:T(128)S(1)} %dynamic_slice.40, s32[32]{0:T(128)S(1)} %dynamic_slice.41), kind=kOutput, calls=%fused_computation.3.clone.1 | convolution fusion | flops 809502720 | bytes 25166080 | tf_op jit(solution)/shard_map/while/body/eval_jaxpr/dot_general | solution.py:47
  399.6 0.1 compare_and_fusion.2
  399.7 10.1 %gather_fusion = f32[32,128,512]{2,1,0:T(8,128)} fusion(f32[64,128,512]{2,1,0:T(8,128)} %get-tuple-element.262, s32[1024]{0:T(1024)S(1)} %pad_clamp_fusion.3), kind=kCustom, calls=%fused_computation.clone.clone.1 | custom fusion | bytes 16777344 | tf_op jit(solution)/shard_map/while/body/eval_jaxpr/jit(_take)/gather | solution.py:42
  409.8 10.9 %fusion.34 = f32[32,128,512]{2,1,0:T(8,128)S(1)} fusion(f32[32,128,512]{2,1,0:T(8,128)} %gather_fusion, pred[32]{0:T(512)(128)(4,1)S(1)} %get-tuple-element.233, f32[128,128,128]{2,1,0:T(8,128)} %get-tuple-element.260, s32[]{:T(128)S(6)} %select_n.79), kind=kOutput, calls=%fused_computation.4.clone.1 | convolution fusion | flops 3223322624 | bytes 18874404 | tf_op jit(solution)/shard_map/while/body/eval_jaxpr/tpq,tqf->tpf/dot_general | solution.py:43
  420.7 8.1 %copy.15 = f32[4,8,128,512]{3,1,2,0:T(8,128)} copy(f32[4,8,128,512]{3,2,1,0:T(8,128)S(1)} %bitcast.34) | data formatting | bytes 16777216 | tf_op jit(solution)/shard_map/while
  428.8 0.1 dynamic_slice.40
  428.9 0.1 dynamic_slice.41
  428.9 13.1 %convolution_add_fusion.3 = f32[32,65536]{1,0:T(8,128)} fusion(f32[32,65536]{1,0:T(8,128)} %bitcast.35, f32[32,65536]{1,0:T(8,128)} %get-tuple-element.246, pred[]{:T(512)S(6)} %compare.5, f32[32]{0:T(128)S(1)} %dynamic_slice.40, s32[32]{0:T(128)S(1)} %dynamic_slice.41), kind=kOutput, calls=%fused_computation.3.clone.1 | convolution fusion | flops 809502720 | bytes 25166080 | tf_op jit(solution)/shard_map/while/body/eval_jaxpr/dot_general | solution.py:47
  442.1 7.5 %reshape.60 = f32[4096,512]{1,0:T(8,128)} reshape(f32[32,65536]{1,0:T(8,128)} %get-tuple-element.144) | data formatting | bytes 16777216 | tf_op jit(solution)/shard_map/reshape | solution.py:55
  449.5 0.0 reduce-scatter.2.cloned.1.call-update
  449.6 50.8 %reduce-scatter.2.cloned.1.call-done = f32[512,512]{1,0:T(8,128)} async-done(((f32[4096,512]{1,0:T(8,128)}), f32[512,512]{1,0:T(8,128)}) %reduce-scatter.2.cloned.1.call-update) | async-done | bytes 1048592 | tf_op jit(solution)/shard_map/reduce_scatter | solution.py:54
  500.4 0.0 copy-done
  500.4 0.0 copy-done.1
  500.4 0.0 copy-done.3
  500.4 0.0 copy-done.4
  500.4 5.1 fusion.14
  (15 shorter events, 0.1 us)
Async XLA Ops:
  6.5 493.9 %copy-start = (bf16[2048,512]{1,0:T(8,128)(2,1)S(1)}, bf16[2048,512]{1,0:T(8,128)(2,1)}, u32[]{:S(2)}) copy-start(bf16[2048,512]{1,0:T(8,128)(2,1)} %param.20) | copy-start | bytes 6291460
  15.8 8.8 %copy-start.2 = (s32[1,1,16,2]{2,3,1,0:T(2,128)S(1)}, s32[1,1,16,2]{2,3,1,0:T(2,128)}, u32[]{:S(2)}) copy-start(s32[1,1,16,2]{2,3,1,0:T(2,128)} %param.17) | copy-start | bytes 388
  15.8 9.7 %copy-start.5 = (s32[1,1,128]{2,1,0:T(1,128)S(1)}, s32[1,1,128]{2,1,0:T(1,128)}, u32[]{:S(2)}) copy-start(s32[1,1,128]{2,1,0:T(1,128)} %param.15) | copy-start | bytes 1540
  15.8 257.9 %copy-start.6 = (s32[1,1,128]{2,1,0:T(1,128)S(1)}, s32[1,1,128]{2,1,0:T(1,128)}, u32[]{:S(2)}) copy-start(s32[1,1,128]{2,1,0:T(1,128)} %param.14) | copy-start | bytes 1540
  15.8 257.9 %all-to-all-start = ((f32[16,4,128,512]{3,2,1,0:T(8,128)}), f32[16,4,128,512]{3,2,1,0:T(8,128)}, u32[]{:S(2)}, u32[]{:S(2)}) async-start(f32[16,4,128,512]{3,2,1,0:T(8,128)} %stack.3), calls=%async_computation | async-start | bytes 33554432 | tf_op jit(solution)/shard_map/all_to_all | solution.py:26
  24.6 475.8 %reduce-scatter.2.cloned.1.call-start = ((), (), s32[]{:S(2)}) async-start(), calls=%async_computation.2 | async-start | bytes 9437184 | tf_op jit(solution)/shard_map/reduce_scatter | solution.py:54
  449.5 50.9 %copy-start.1 = (f32[512,512]{1,0:T(8,128)S(1)}, f32[512,512]{1,0:T(8,128)}, u32[]{:S(2)}) copy-start(f32[512,512]{1,0:T(8,128)} %param.12) | copy-start | bytes 3145732
  449.5 50.9 %copy-start.3 = (f32[2048]{0:T(1024)S(1)}, f32[2048]{0:T(1024)}, u32[]{:S(2)}) copy-start(f32[2048]{0:T(1024)} %param.19) | copy-start | bytes 24580
  449.5 50.9 %copy-start.4 = (f32[512]{0:T(512)S(1)}, f32[512]{0:T(512)}, u32[]{:S(2)}) copy-start(f32[512]{0:T(512)} %param.21) | copy-start | bytes 6148
Sparse Core Ops, SparseCore 0:
  449.7 50.6 reduce-scatter.1
